TPU v7x, 32 devices: a whole 2x2x4 slice. The times are simulated.
32 devices in a mesh: rep: 2 (over x), fsdp: 16 (over z, y, core).
Axes of the slice: x: 2, y: 2, z: 4, core: 2. Of those that a mesh axis runs over, the one named last changes fastest.
Arguments:
- tokens: bfloat16 [4, 1024, 2048], P('rep', 'fsdp'), may hold values from -6 to 6
- segment_ids: int32 [4, 1024], P('rep', 'fsdp'), may hold values from 0 to 1, never falling along the last dimension, each value on 1 to 768 neighbouring positions
- norm_gains: bfloat16 [2048, 2], P('fsdp'), may hold values from 0.5 to 1.5
- attn_weight: bfloat16 [2048, 4608], P('fsdp'), may hold values from -0.79549513 to 0.79549513
- adapter: bfloat16 [2048, 768], P('fsdp'), may hold values from -0.125 to 0.125
- ffn_weight: bfloat16 [16384, 3, 2048], P('fsdp'), may hold values from -0.125 to 0.125
- ffn_adapter: bfloat16 [16384, 256], P('fsdp'), may hold values from -0.046875 to 0.046875
- cotangent: bfloat16 [4, 1024, 2048], P('rep', 'fsdp'), may hold values from -6 to 6
Outputs:
- block_output: bfloat16 [4, 1024, 2048], P('rep', 'fsdp')
- input_grad: bfloat16 [4, 1024, 2048], P('rep', 'fsdp')
- gains_grad: float32 [2048, 2], P('fsdp')
- attn_grad: float32 [2048, 4608], P('fsdp')
- adapter_grad: float32 [2048, 768], P('fsdp')
- ffn_grad: float32 [16384, 3, 2048], P('fsdp')
- ffn_adapter_grad: float32 [16384, 256], P('fsdp')
Inputs may be any that keep to these rules, and one draw needn't show every extreme that they name: `segment_ids`: in each sequence the ids never fall and each id of 0 to 1 marks one document of 1 to 768 tokens.
All inputs are finite; a program needn't handle non-finite values.
Results may differ from a plain program's by a relative error of at most 0.019.
Values may be sent and summed in bfloat16 or wider, within the bound.
A program may use at most 448 MiB of HBM per device.

v0:
```python
import jax
import jax.numpy as jnp
from jax import lax
from jax.sharding import PartitionSpec as P

HEADS = 8
HD = 256
RANK = 256
CHUNKS = 4
epsilon = 1e-06


def rms_scale(values, gain_col):
    return (
        values * lax.rsqrt(jnp.mean(values * values, axis=-1, keepdims=True) + epsilon) * gain_col
    )


def angles_of(positions):
    inverse_freq = 10000.0 ** (-2.0 * jnp.arange(HD // 2, dtype=jnp.float32) / HD)
    return positions.astype(jnp.float32)[..., None] * inverse_freq


def rotate(field_in, angles):
    half_dim = field_in.shape[-1] // 2
    cosine = jnp.cos(angles)
    sine_part = jnp.sin(angles)
    lower_half = field_in[..., :half_dim]
    upper_half = field_in[..., half_dim:]
    return jnp.concatenate(
        [
            lower_half * cosine - upper_half * sine_part,
            upper_half * cosine + lower_half * sine_part,
        ],
        axis=-1,
    )


def gelu_tanh(values):
    return jax.nn.gelu(values, approximate=True)


def contract(left_op, right_op, left_dim, right_dim):
    return lax.dot_general(
        left_op,
        right_op,
        (((left_dim,), (right_dim,)), ((), ())),
        preferred_element_type=jnp.float32,
    )


def batched(left_op, right_op, left_dim, right_dim):
    return lax.dot_general(
        left_op,
        right_op,
        (((left_dim,), (right_dim,)), ((0,), (0,))),
        preferred_element_type=jnp.float32,
    )


def low(values):
    return values.astype(jnp.bfloat16)


def gather_rows(values):
    return lax.all_gather(values, "fsdp", axis=values.ndim - 2, tiled=True)


def sum_rows(values):
    return lax.psum_scatter(values, "fsdp", scatter_dimension=1, tiled=True)


def swap_rep(values):
    return lax.ppermute(values, "rep", [(0, 1), (1, 0)])


def local(
    tokens, segment_ids, norm_gains, attn_weight, adapter, ffn_weight, ffn_adapter, cotangent
):
    micro, local_len, model_dim = tokens.shape
    shards = lax.axis_size("fsdp")
    me = lax.axis_index("fsdp")
    seq_len = local_len * shards
    offset = me * local_len
    count = micro * local_len
    every = micro * seq_len
    q_width = HEADS * HD
    kv_end = q_width + 2 * HD
    score_scale = HD ** (-0.5)
    hidden_cols = ffn_weight.shape[0]
    attn_rows = attn_weight.shape[0]
    seg_cols = count // attn_rows
    seg_block = low(segment_ids).reshape(attn_rows, seg_cols)
    spare = jnp.zeros((attn_rows, 128 - 2 - seg_cols), jnp.bfloat16)
    first = gather_rows(
        jnp.concatenate(
            [attn_weight[:, :kv_end], adapter[:, : 2 * RANK], norm_gains, seg_block, spare], axis=1
        )
    )
    second = gather_rows(jnp.concatenate([attn_weight[:, kv_end:], adapter[:, 2 * RANK :]], axis=1))
    extra = kv_end + 2 * RANK
    w_proj = first[:, :kv_end]
    a_q = first[:, kv_end : kv_end + RANK]
    bq_t = first[:, kv_end + RANK : extra]
    gain_two = first[:, extra : extra + 2].astype(jnp.float32)
    seg_all = first[:, extra + 2 : extra + 2 + seg_cols].reshape(shards, micro, local_len)
    seg_all = seg_all.transpose(1, 0, 2).reshape(micro, seq_len).astype(jnp.int32)
    w_out = second[:, :q_width]
    bd_t = second[:, q_width:]
    cot_all = gather_rows(cotangent).reshape(every, model_dim)
    hidden_in = tokens.reshape(count, model_dim).astype(jnp.float32)
    key_index = jnp.arange(seq_len, dtype=jnp.int32)
    query_index = offset + jnp.arange(local_len, dtype=jnp.int32)
    before = jnp.sum((seg_all[:, None, :] < segment_ids[:, :, None]).astype(jnp.int32), axis=2)
    angles = angles_of(query_index[None, :] - before).reshape(count, HD // 2)
    normed, norm_back_one = jax.vjp(rms_scale, hidden_in, gain_two[:, 0])
    normed_low = low(normed)
    normed_cols = lax.all_to_all(
        normed_low.reshape(micro, local_len, model_dim), "fsdp", 2, 1, tiled=True
    ).reshape(every, attn_rows)
    projected = contract(normed_low, w_proj, 1, 0)
    query_low = low(contract(normed_low, a_q, 1, 0))
    query_pre = projected[:, :q_width] + contract(query_low, bq_t, 1, 1)
    queries = low(rotate(query_pre.reshape(count, HEADS, HD), angles[:, None, :]))
    queries = queries.reshape(micro, local_len * HEADS, HD)
    keys_low = low(rotate(projected[:, q_width : q_width + HD], angles))
    values_low = low(projected[:, q_width + HD :])
    kv_all = gather_rows(
        jnp.concatenate([keys_low, values_low], axis=1).reshape(micro, local_len, 2 * HD)
    )
    keys_all = kv_all[..., :HD]
    values_all = kv_all[..., HD:]
    allowed = (
        (segment_ids[:, :, None] == seg_all[:, None, :])
        & (key_index[None, None, :] <= query_index[None, :, None])
    )[:, :, None, :]
    scores = (batched(queries, keys_all, 2, 2) * score_scale).reshape(
        micro, local_len, HEADS, seq_len
    )
    scores = jnp.where(allowed, scores, -1e30)
    top_score = jnp.max(scores, axis=-1, keepdims=True)
    exp_scores = jnp.exp(scores - top_score)
    weights = exp_scores / jnp.sum(exp_scores, axis=-1, keepdims=True)
    weights_low = low(weights).reshape(micro, local_len * HEADS, seq_len)
    context = low(batched(weights_low, values_all, 2, 1)).reshape(count, q_width)
    mixed_sum = hidden_in + contract(context, w_out, 1, 1)
    normed_two, norm_back_two = jax.vjp(rms_scale, mixed_sum, gain_two[:, 1])
    inputs_all = gather_rows(low(normed_two).reshape(micro, local_len, model_dim))
    inputs_all = inputs_all.reshape(every, model_dim)
    kept_all = gather_rows(
        jnp.concatenate([context, query_low], axis=1).reshape(micro, local_len, q_width + RANK)
    ).reshape(every, q_width + RANK)
    low_grad_all = low(contract(cot_all, bd_t, 1, 0))
    step = hidden_cols // CHUNKS
    hidden_parts, gate_parts, up_parts, ffn_parts, low_parts = ([], [], [], [], [])
    for at in range(CHUNKS):
        units = slice(at * step, (at + 1) * step)
        w_gate, w_up, w_down = (ffn_weight[units, j, :] for j in range(3))
        gate_pre = contract(inputs_all, w_gate, 1, 1)
        up_pre = contract(inputs_all, w_up, 1, 1)
        activated, gelu_back = jax.vjp(gelu_tanh, gate_pre)
        hidden_act = low(activated * up_pre)
        hidden_grad = contract(cot_all, w_down, 1, 1) + contract(
            low_grad_all, ffn_adapter[units], 1, 1
        )
        gate_grad = low(gelu_back(hidden_grad * up_pre)[0])
        up_grad = low(hidden_grad * activated)
        mine = low(
            jnp.stack(
                [
                    contract(gate_grad, inputs_all, 0, 0),
                    contract(up_grad, inputs_all, 0, 0),
                    contract(hidden_act, cot_all, 0, 0),
                ],
                axis=0,
            )
        )
        mine_low = low(contract(hidden_act, low_grad_all, 0, 0))
        ffn_parts.append((mine, swap_rep(mine)))
        low_parts.append((mine_low, swap_rep(mine_low)))
        hidden_parts.append(hidden_act)
        gate_parts.append(gate_grad)
        up_parts.append(up_grad)
    gate_grad = jnp.concatenate(gate_parts, axis=1)
    up_grad = jnp.concatenate(up_parts, axis=1)
    hidden_act = jnp.concatenate(hidden_parts, axis=1)
    normed_two_grad = sum_rows(
        low(
            contract(gate_grad, ffn_weight[:, 0, :], 1, 0)
            + contract(up_grad, ffn_weight[:, 1, :], 1, 0)
        ).reshape(micro, seq_len, model_dim)
    )
    normed_two_grad = normed_two_grad.reshape(count, model_dim).astype(jnp.float32)
    down_mine = sum_rows(
        jnp.concatenate(
            [
                low(contract(hidden_act, ffn_weight[:, 2, :], 1, 0)),
                low(contract(hidden_act, ffn_adapter, 1, 0)),
            ],
            axis=1,
        ).reshape(micro, seq_len, model_dim + RANK)
    ).reshape(count, model_dim + RANK)
    down_low = down_mine[:, model_dim:]
    result = (
        mixed_sum + down_mine[:, :model_dim].astype(jnp.float32) + contract(down_low, bd_t, 1, 1)
    )
    cot_full = cotangent.reshape(count, model_dim).astype(jnp.float32)
    mixed_part, gain_two_grad = norm_back_two(normed_two_grad)
    mixed_grad = cot_full + mixed_part
    out_grad_low = low(mixed_grad)
    out_cols = lax.all_to_all(
        out_grad_low.reshape(micro, local_len, model_dim), "fsdp", 2, 1, tiled=True
    ).reshape(every, attn_rows)
    wout_grad = contract(out_cols, kept_all[:, :q_width], 0, 0)
    context_grad = contract(out_grad_low, w_out, 1, 0)
    context_rows = low(context_grad).reshape(micro, local_len * HEADS, HD)
    prob_grad = batched(context_rows, values_all, 2, 2).reshape(micro, local_len, HEADS, seq_len)
    score_grad = weights * (prob_grad - jnp.sum(weights * prob_grad, axis=-1, keepdims=True))
    score_grad = low(score_grad).reshape(micro, local_len * HEADS, seq_len)
    query_grad = batched(score_grad, keys_all, 2, 1) * score_scale
    query_grad = query_grad.reshape(count, HEADS, HD)
    kv_grad = sum_rows(
        low(
            jnp.concatenate(
                [
                    batched(score_grad, queries, 1, 1) * score_scale,
                    batched(weights_low, context_rows, 1, 1),
                ],
                axis=2,
            )
        )
    ).reshape(count, 2 * HD)
    query_pre_grad = low(rotate(query_grad, -angles[:, None, :]).reshape(count, q_width))
    key_grad = low(rotate(kv_grad[:, :HD].astype(jnp.float32), -angles))
    value_grad = kv_grad[:, HD:]
    rank_grad = low(contract(query_pre_grad, bq_t, 1, 0))
    proj_grad = jnp.concatenate([query_pre_grad, key_grad, value_grad], axis=1)
    normed_grad = contract(proj_grad, w_proj, 1, 1) + contract(rank_grad, a_q, 1, 1)
    hidden_part, gain_one_grad = norm_back_one(normed_grad)
    input_grad = low(mixed_grad + hidden_part)
    back_all = gather_rows(
        jnp.concatenate([proj_grad, rank_grad, down_low], axis=1).reshape(
            micro, local_len, kv_end + 2 * RANK
        )
    ).reshape(every, kv_end + 2 * RANK)
    my_cols = me * attn_rows
    attn_in = contract(normed_cols, back_all[:, : kv_end + RANK], 0, 0)
    bq_grad = contract(
        lax.dynamic_slice_in_dim(back_all, my_cols, attn_rows, 1), kept_all[:, q_width:], 0, 0
    )
    bd_grad = contract(
        lax.dynamic_slice_in_dim(cot_all, my_cols, attn_rows, 1), back_all[:, kv_end + RANK :], 0, 0
    )
    gain_now = jnp.stack([gain_one_grad, gain_two_grad], axis=1).reshape(shards, attn_rows, 2)
    gain_now = lax.all_to_all(gain_now, "fsdp", 0, 0, tiled=True).sum(axis=0)
    tail = low(jnp.concatenate([attn_in, bq_grad, bd_grad], axis=1))
    tail_out = low(wout_grad)
    tail_gain = low(gain_now)

    def total(mine, other):
        return mine.astype(jnp.float32) + other.astype(jnp.float32)

    tail = total(tail, swap_rep(tail))
    tail_out = total(tail_out, swap_rep(tail_out))
    gains_grad = total(tail_gain, swap_rep(tail_gain))
    attn_grad = jnp.concatenate([tail[:, :kv_end], tail_out], axis=1)
    adapter_grad = tail[:, kv_end:]
    ffn_grad = jnp.concatenate([total(*pair) for pair in ffn_parts], axis=1).transpose(1, 0, 2)
    ffn_low_grad = jnp.concatenate([total(*pair) for pair in low_parts], axis=0)
    return (
        low(result).reshape(micro, local_len, model_dim),
        input_grad.reshape(micro, local_len, model_dim),
        gains_grad,
        attn_grad,
        adapter_grad,
        ffn_grad,
        ffn_low_grad,
    )


def solution(mesh):
    placed = (
        P("rep", "fsdp", None),
        P("rep", "fsdp"),
        P("fsdp", None),
        P("fsdp", None),
        P("fsdp", None),
        P("fsdp", None, None),
        P("fsdp", None),
        P("rep", "fsdp", None),
    )
    return jax.shard_map(
        local,
        mesh=mesh,
        in_specs=placed,
        out_specs=(
            P("rep", "fsdp", None),
            P("rep", "fsdp", None),
            P("fsdp", None),
            P("fsdp", None),
            P("fsdp", None),
            P("fsdp", None, None),
            P("fsdp", None),
        ),
        check_vma=False,
    )
```

profile of v0, /device:TPU:0, one launch (start us, length us, event | category | flops | bytes accessed | tf_op | source)
XLA Modules:
  0.0 1266.3 jit_solution(10089645762833557371)
XLA Ops:
  13.1 105.5 %all-gather.8.cloned.1.call-done = bf16[2048,3200]{1,0:T(8,128)(2,1)} async-done(((bf16[128,3200]{1,0:T(8,128)(2,1)}), bf16[2048,3200]{1,0:T(8,128)(2,1)}) %all-gather.8.cloned.1.call-update) | async-done | bytes 13107216 | tf_op jit(solution)/shard_map/all_gather | solution.py:66
  136.6 34.2 %all-gather.10.cloned.1.call-done = bf16[2,1024,512]{2,1,0:T(8,128)(2,1)} async-done(((bf16[2,64,512]{2,1,0:T(8,128)(2,1)}), bf16[2,1024,512]{2,1,0:T(8,128)(2,1)}) %all-gather.10.cloned.1.call-update) | async-done | bytes 2097168 | tf_op jit(solution)/shard_map/all_gather | solution.py:66
  178.1 75.3 %all-gather.12.cloned.1.call-done = bf16[2048,2304]{1,0:T(8,128)(2,1)} async-done(((bf16[128,2304]{1,0:T(8,128)(2,1)}), bf16[2048,2304]{1,0:T(8,128)(2,1)}) %all-gather.12.cloned.1.call-update) | async-done | bytes 9437200 | tf_op jit(solution)/shard_map/all_gather | solution.py:66
  253.4 6.4 multiply_reduce_fusion.1
  261.6 66.7 %all-gather.16.cloned.1.call-done = bf16[2,1024,2048]{2,1,0:T(8,128)(2,1)} async-done(((bf16[2,64,2048]{2,1,0:T(8,128)(2,1)}), bf16[2,1024,2048]{2,1,0:T(8,128)(2,1)}) %all-gather.16.cloned.1.call-update) | async-done | bytes 8388624 | tf_op jit(solution)/shard_map/all_gather | solution.py:66
  328.2 7.5 fusion.100
  354.1 49.7 %all-gather.14.cloned.1.call-done = bf16[2,1024,2048]{2,1,0:T(8,128)(2,1)} async-done(((bf16[2,64,2048]{2,1,0:T(8,128)(2,1)}), bf16[2,1024,2048]{2,1,0:T(8,128)(2,1)}) %all-gather.14.cloned.1.call-update) | async-done | bytes 8388624 | tf_op jit(solution)/shard_map/all_gather | solution.py:66
  403.8 7.6 fusion.110
  411.4 7.4 fusion.108
  450.8 14.4 %fusion.13 = f32[2048,2048]{1,0:T(8,128)} fusion(bf16[2048,256]{0,1:T(8,128)(2,1)} %get-tuple-element.27, bf16[2048,256]{0,1:T(8,128)(2,1)} %get-tuple-element.24, bf16[2048,256]{0,1:T(8,128)(2,1)} %get-tuple-element.21, bf16[2048,256]{0,1:T(8,128)(2,1)} %get-tuple-element.18, bf16[1024,3,2048]{2,0,1:T(8,128)(2,1)S(1)} %bitcast.272), kind=kOutput, calls=%fused_computation.22 | convolution fusion | flops 8606711808 | bytes 25165824 | tf_op jit(solution)/shard_map/dot_general | solution.py:44
  465.2 16.5 %add_convert_fusion = bf16[2048,2048]{1,0:T(8,128)(2,1)} fusion(f32[2048,2048]{1,0:T(8,128)} %fusion.13, bf16[2048,256]{0,1:T(8,128)(2,1)} %get-tuple-element.26, bf16[2048,256]{0,1:T(8,128)(2,1)} %get-tuple-element.23, bf16[2048,256]{0,1:T(8,128)(2,1)} %get-tuple-element.20, bf16[2048,256]{0,1:T(8,128)(2,1)S(1)} %copy-done.65, bf16[1024,3,2048]{2,0,1:T(8,128)(2,1)} %param.13), kind=kOutput, calls=%fused_computation.2 | convolution fusion | flops 8615100416 | bytes 33554432 | tf_op jit(solution)/shard_map/dot_general | solution.py:44
  481.7 13.9 %convolution_convert_fusion = bf16[2048,2048]{0,1:T(8,128)(2,1)} fusion(bf16[1024,3,2048]{2,0,1:T(8,128)(2,1)} %param.13, bf16[2048,256]{0,1:T(8,128)(2,1)S(1)} %get-tuple-element.28, bf16[2048,256]{0,1:T(8,128)(2,1)} %get-tuple-element.25, bf16[2048,256]{0,1:T(8,128)(2,1)} %get-tuple-element.22, bf16[2048,256]{0,1:T(8,128)(2,1)} %get-tuple-element.19), kind=kOutput, calls=%fused_computation.12 | convolution fusion | flops 8610906112 | bytes 16777216 | tf_op jit(solution)/shard_map/dot_general | solution.py:44
  495.6 88.2 %reduce-scatter.5.cloned.1.call-done = bf16[2,64,2048]{2,1,0:T(8,128)(2,1)} async-done(((bf16[2,1024,2048]{2,1,0:T(8,128)(2,1)}), bf16[2,64,2048]{2,1,0:T(8,128)(2,1)}) %reduce-scatter.5.cloned.1.call-update) | async-done | bytes 524304 | tf_op jit(solution)/shard_map/reduce_scatter | solution.py:70
  608.6 11.2 pad_maximum_fusion
  619.8 12.7 %copy.70 = bf16[2048,2304]{1,0:T(8,128)(2,1)} copy(bf16[2048,2304]{0,1:T(8,128)(2,1)} %pad_maximum_fusion) | data formatting | bytes 18874368 | tf_op jit(solution)/shard_map/reshape | solution.py:201
  638.4 64.7 %all-reduce.3.cloned.1.call-done = bf16[2,1024,512]{2,0,1:T(2,128)(2,1)} async-done(((bf16[2,1024,512]{2,0,1:T(2,128)(2,1)}), bf16[2,1024,512]{2,0,1:T(2,128)(2,1)}) %all-reduce.3.cloned.1.call-update) | async-done | bytes 2097168
  707.6 110.2 %reduce-scatter.3.cloned.1.call-done = bf16[2,64,2304]{2,1,0:T(8,128)(2,1)} async-done(((bf16[2,1024,2304]{2,1,0:T(8,128)(2,1)}), bf16[2,64,2304]{2,1,0:T(8,128)(2,1)}) %reduce-scatter.3.cloned.1.call-update) | async-done | bytes 589840 | tf_op jit(solution)/shard_map/reduce_scatter | solution.py:70
  826.5 21.9 %all-to-all-done.1 = bf16[16,2,8192]{2,1,0:T(2,128)(2,1)S(1)} async-done(((bf16[16,2,8192]{2,1,0:T(2,128)(2,1)}), bf16[16,2,8192]{2,1,0:T(2,128)(2,1)S(1)}, u32[]{:S(2)}, u32[]{:S(2)}) %all-to-all-start.1) | async-done | bytes 524320 | tf_op jit(solution)/shard_map/all_to_all | solution.py:118
  849.8 6.2 fusion.49
  856.0 5.9 fusion.48
  881.5 5.9 fusion.43
  893.3 6.1 fusion.41
  901.1 5.9 fusion.40
  907.0 6.1 fusion.39
  925.0 148.4 %collective-permute-done.10 = bf16[256,256]{1,0:T(8,128)(2,1)S(1)} collective-permute-done((bf16[256,256]{1,0:T(8,128)(2,1)S(1)}, bf16[256,256]{1,0:T(8,128)(2,1)S(1)}, u32[]{:S(2)}, u32[]{:S(2)}) %collective-permute-start.10) | collective-permute-done | bytes 131104 | tf_op jit(solution)/shard_map/ppermute | solution.py:74
  1074.8 67.5 %collective-permute-done.9 = bf16[256,256]{1,0:T(8,128)(2,1)S(1)} collective-permute-done((bf16[256,256]{1,0:T(8,128)(2,1)S(1)}, bf16[256,256]{1,0:T(8,128)(2,1)S(1)}, u32[]{:S(2)}, u32[]{:S(2)}) %collective-permute-start.9) | collective-permute-done | bytes 131104 | tf_op jit(solution)/shard_map/ppermute | solution.py:74
  1168.5 8.6 all-to-all-start.2
  1177.1 17.8 %maximum_bitcast_fusion = f32[1024,3,2048]{2,0,1:T(8,128)} fusion(f32[3,256,2048]{2,1,0:T(8,128)} %convert_add_fusion, f32[3,256,2048]{2,1,0:T(8,128)} %convert_add_fusion.1, f32[3,256,2048]{2,1,0:T(8,128)} %convert_add_fusion.2, f32[3,256,2048]{2,1,0:T(8,128)} %convert_add_fusion.3), kind=kLoop, calls=%fused_computation.1 | loop fusion | flops 18874368 | bytes 50331648 | tf_op jit(solution)/shard_map/transpose | solution.py:268
  1203.3 6.2 fusion.3
  1213.1 6.3 all-to-all-start
  1230.1 6.0 fusion.34
  1242.2 14.3 %collective-permute-done.1 = bf16[128,3328]{1,0:T(8,128)(2,1)S(1)} collective-permute-done((bf16[128,3328]{1,0:T(8,128)(2,1)S(1)}, bf16[128,3328]{1,0:T(8,128)(2,1)S(1)}, u32[]{:S(2)}, u32[]{:S(2)}) %collective-permute-start.1) | collective-permute-done | bytes 852000 | tf_op jit(solution)/shard_map/ppermute | solution.py:74
  (349 shorter events, 224.8 us)
Async XLA Ops:
  7.2 111.4 %all-gather.8.cloned.1.call-start = ((), (), s32[]{:S(2)}) async-start(), calls=%async_computation.5 | async-start | bytes 13926400 | tf_op jit(solution)/shard_map/all_gather | solution.py:66
  12.1 158.8 %all-gather.10.cloned.1.call-start = ((), (), s32[]{:S(2)}) async-start(), calls=%async_computation.6 | async-start | bytes 2228224 | tf_op jit(solution)/shard_map/all_gather | solution.py:66
  13.1 116.0 %copy-start.43 = (f32[128]{0:T(128)}, f32[128]{0:T(128)S(1)}, u32[]{:S(2)}) copy-start(f32[128]{0:T(128)S(1)} %multiply_power_fusion) | copy-start | bytes 1540
  120.6 465.1 %copy-start.33 = (f32[2048]{0:T(1024)}, f32[2048]{0:T(1024)S(1)}, u32[]{:S(2)}) copy-start(f32[2048]{0:T(1024)S(1)} %get-tuple-element.11) | copy-start | bytes 24580
  131.0 122.4 %all-gather.12.cloned.1.call-start = ((), (), s32[]{:S(2)}) async-start(), calls=%async_computation.7 | async-start | bytes 10027008 | tf_op jit(solution)/shard_map/all_gather | solution.py:66
  131.9 196.3 %all-gather.16.cloned.1.call-start = ((), (), s32[]{:S(2)}) async-start(), calls=%async_computation.10 | async-start | bytes 8912896 | tf_op jit(solution)/shard_map/all_gather | solution.py:66
  132.5 271.2 %all-gather.14.cloned.1.call-start = ((), (), s32[]{:S(2)}) async-start(), calls=%async_computation.8 | async-start | bytes 8912896 | tf_op jit(solution)/shard_map/all_gather | solution.py:66
  259.7 326.0 %copy-start = (f32[128,2048]{1,0:T(8,128)}, f32[128,2048]{1,0:T(8,128)S(1)}, u32[]{:S(2)}) copy-start(f32[128,2048]{1,0:T(8,128)S(1)} %get-tuple-element.48) | copy-start | bytes 3145732
  259.8 326.0 %copy-start.41 = (f32[128]{0:T(128)}, f32[128]{0:T(128)S(1)}, u32[]{:S(2)}) copy-start(f32[128]{0:T(128)S(1)} %fusion.176) | copy-start | bytes 1540
  261.0 322.8 %reduce-scatter.5.cloned.1.call-start = ((), (), s32[]{:S(2)}) async-start(), calls=%async_computation.11 | async-start | bytes 8912896 | tf_op jit(solution)/shard_map/reduce_scatter | solution.py:70
  440.6 164.6 %copy-start.18 = (bf16[2048,256]{0,1:T(8,128)(2,1)}, bf16[2048,256]{0,1:T(8,128)(2,1)S(1)}, u32[]{:S(2)}) copy-start(bf16[2048,256]{0,1:T(8,128)(2,1)S(1)} %get-tuple-element.28) | copy-start | bytes 3145732
  481.7 221.4 %all-reduce.3.cloned.1.call-start = ((), (), s32[]{:S(2)}) async-start(), calls=%async_computation.14 | async-start | bytes 4194304
  605.2 212.6 %reduce-scatter.3.cloned.1.call-start = ((), (), s32[]{:S(2)}) async-start(), calls=%async_computation.9 | async-start | bytes 10027008 | tf_op jit(solution)/shard_map/reduce_scatter | solution.py:70
  632.6 563.8 %all-gather.20.cloned.1.call-start = ((), (), s32[]{:S(2)}) async-start(), calls=%async_computation.13 | async-start | bytes 10027008 | tf_op jit(solution)/shard_map/all_gather | solution.py:66
  634.7 591.8 %all-gather.18.cloned.1.call-start = ((), (), s32[]{:S(2)}) async-start(), calls=%async_computation.12 | async-start | bytes 13369344 | tf_op jit(solution)/shard_map/all_gather | solution.py:66
  638.0 181.6 %copy-start.5 = (bf16[2,64,2048]{2,1,0:T(8,128)(2,1)S(1)}, bf16[2,64,2048]{2,1,0:T(8,128)(2,1)}, u32[]{:S(2)}) copy-start(bf16[2,64,2048]{2,1,0:T(8,128)(2,1)} %param.8) | copy-start | bytes 1572868
  638.0 181.6 %copy-start.36 = (f32[2048]{0:T(1024)S(1)}, f32[2048]{0:T(1024)}, u32[]{:S(2)}) copy-start(f32[2048]{0:T(1024)} %copy-done.35) | copy-start | bytes 24580
  638.0 181.6 %copy-start.52 = (f32[2,64]{1,0:T(2,128)S(1)}, f32[2,64]{1,0:T(2,128)}, u32[]{:S(2)}) copy-start(f32[2,64]{1,0:T(2,128)} %get-tuple-element.37) | copy-start | bytes 1540
  822.1 26.2 %all-to-all-start.1 = ((bf16[16,2,8192]{2,1,0:T(2,128)(2,1)}), bf16[16,2,8192]{2,1,0:T(2,128)(2,1)S(1)}, u32[]{:S(2)}, u32[]{:S(2)}) async-start(bf16[16,2,8192]{2,1,0:T(2,128)(2,1)} %reshape.417), calls=%async_computation.3 | async-start | bytes 1048576 | tf_op jit(solution)/shard_map/all_to_all | solution.py:118
  864.7 288.7 %collective-permute-start.6 = (bf16[3,256,2048]{2,1,0:T(8,128)(2,1)S(1)}, bf16[3,256,2048]{2,1,0:T(8,128)(2,1)S(1)}, u32[]{:S(2)}, u32[]{:S(2)}) collective-permute-start(bf16[3,256,2048]{2,1,0:T(8,128)(2,1)S(1)} %pad_maximum_fusion.5), channel_id=1, source_target_pairs={{0,16},{16,0},{1,17},{17,1},{2,18},{18,2},{3,19},{19,3},{4,20},{20... | collective-permute-start | bytes 9437192 | tf_op jit(solution)/shard_map/ppermute | solution.py:74
  880.6 276.0 %collective-permute-start.5 = (bf16[3,256,2048]{2,1,0:T(8,128)(2,1)S(1)}, bf16[3,256,2048]{2,1,0:T(8,128)(2,1)S(1)}, u32[]{:S(2)}, u32[]{:S(2)}) collective-permute-start(bf16[3,256,2048]{2,1,0:T(8,128)(2,1)S(1)} %pad_maximum_fusion.4), channel_id=1, source_target_pairs={{0,16},{16,0},{1,17},{17,1},{2,18},{18,2},{3,19},{19,3},{4,20},{20... | collective-permute-start | bytes 9437192 | tf_op jit(solution)/shard_map/ppermute | solution.py:74
  899.7 260.1 %collective-permute-start.4 = (bf16[3,256,2048]{2,1,0:T(8,128)(2,1)S(1)}, bf16[3,256,2048]{2,1,0:T(8,128)(2,1)S(1)}, u32[]{:S(2)}, u32[]{:S(2)}) collective-permute-start(bf16[3,256,2048]{2,1,0:T(8,128)(2,1)S(1)} %pad_maximum_fusion.3), channel_id=1, source_target_pairs={{0,16},{16,0},{1,17},{17,1},{2,18},{18,2},{3,19},{19,3},{4,20},{20... | collective-permute-start | bytes 9437192 | tf_op jit(solution)/shard_map/ppermute | solution.py:74
  920.6 152.8 %collective-permute-start.10 = (bf16[256,256]{1,0:T(8,128)(2,1)S(1)}, bf16[256,256]{1,0:T(8,128)(2,1)S(1)}, u32[]{:S(2)}, u32[]{:S(2)}) collective-permute-start(bf16[256,256]{1,0:T(8,128)(2,1)S(1)} %convolution_convert_fusion.17), channel_id=1, source_target_pairs={{0,16},{16,0},{1,17},{17,1},{2,18},{18,2},{3,19},{19,3},{4,20},{20... | collective-permute-start | bytes 393224 | tf_op jit(solution)/shard_map/ppermute | solution.py:74
  923.5 239.5 %collective-permute-start.3 = (bf16[3,256,2048]{2,1,0:T(8,128)(2,1)S(1)}, bf16[3,256,2048]{2,1,0:T(8,128)(2,1)S(1)}, u32[]{:S(2)}, u32[]{:S(2)}) collective-permute-start(bf16[3,256,2048]{2,1,0:T(8,128)(2,1)S(1)} %pad_maximum_fusion.2), channel_id=1, source_target_pairs={{0,16},{16,0},{1,17},{17,1},{2,18},{18,2},{3,19},{19,3},{4,20},{20... | collective-permute-start | bytes 9437192 | tf_op jit(solution)/shard_map/ppermute | solution.py:74
  1073.3 69.0 %collective-permute-start.9 = (bf16[256,256]{1,0:T(8,128)(2,1)S(1)}, bf16[256,256]{1,0:T(8,128)(2,1)S(1)}, u32[]{:S(2)}, u32[]{:S(2)}) collective-permute-start(bf16[256,256]{1,0:T(8,128)(2,1)S(1)} %convolution_convert_fusion.18), channel_id=1, source_target_pairs={{0,16},{16,0},{1,17},{17,1},{2,18},{18,2},{3,19},{19,3},{4,20},{20... | collective-permute-start | bytes 393224 | tf_op jit(solution)/shard_map/ppermute | solution.py:74
  1142.4 5.0 collective-permute-start.8
  1147.3 5.0 collective-permute-start.7
  1168.5 26.4 %all-to-all-start.2 = ((bf16[16,2,8192]{2,1,0:T(2,128)(2,1)}), bf16[16,2,8192]{2,1,0:T(2,128)(2,1)S(1)}, u32[]{:S(2)}, u32[]{:S(2)}) async-start(bf16[16,2,8192]{2,1,0:T(2,128)(2,1)} %reshape.415), calls=%async_computation.4 | async-start | bytes 1048576 | tf_op jit(solution)/shard_map/all_to_all | solution.py:211
  1201.8 36.4 %collective-permute-start.2 = (bf16[128,2048]{1,0:T(8,128)(2,1)}, bf16[128,2048]{1,0:T(8,128)(2,1)}, u32[]{:S(2)}, u32[]{:S(2)}) collective-permute-start(bf16[128,2048]{1,0:T(8,128)(2,1)} %fusion.56), channel_id=1, source_target_pairs={{0,16},{16,0},{1,17},{17,1},{2,18},{18,2},{3,19},{19,3},{4,20},{20... | collective-permute-start | bytes 1572872 | tf_op jit(solution)/shard_map/ppermute | solution.py:74
  1213.1 12.8 %all-to-all-start = ((f32[16,128,2]{1,2,0:T(2,128)}), f32[16,128,2]{1,2,0:T(2,128)S(1)}, u32[]{:S(2)}, u32[]{:S(2)}) async-start(f32[16,128,2]{1,2,0:T(2,128)} %copy.61), calls=%async_computation.2 | async-start | bytes 32768 | tf_op jit(solution)/shard_map/all_to_all | solution.py:255
  1225.9 11.8 collective-permute-start
  1236.1 20.4 %collective-permute-start.1 = (bf16[128,3328]{1,0:T(8,128)(2,1)S(1)}, bf16[128,3328]{1,0:T(8,128)(2,1)S(1)}, u32[]{:S(2)}, u32[]{:S(2)}) collective-permute-start(bf16[128,3328]{1,0:T(8,128)(2,1)S(1)} %pad_maximum_fusion.9), channel_id=1, source_target_pairs={{0,16},{16,0},{1,17},{17,1},{2,18},{18,2},{3,19},{19,3},{4,20},{20... | collective-permute-start | bytes 2555912 | tf_op jit(solution)/shard_map/ppermute | solution.py:74
  (76 other events, 1120.7 us)
Sparse Core Ops, SparseCore 0:
  12.2 106.3 all-gather.7
  131.1 39.7 all-gather.9
  173.7 79.6 all-gather.11
  255.4 72.7 all-gather.15
  330.8 72.8 all-gather.13
  481.8 101.9 reduce-scatter.4
  605.4 97.6 all-reduce.2
  707.2 110.6 reduce-scatter.2
  820.1 90.3 all-gather.19
  912.7 98.8 all-gather.17
where the time goes:
time: 1280 us; the launch traced here: 1270 us
  waiting for transfers between devices  858 us (67%)
  matrix products  246 us (19%)
  other arithmetic  69.1 us (5%)
  local copies, waits for them, and re-layouts  42.9 us (3%)
  starting transfers between devices  34.2 us (3%)
  between operations  16.7 us (1%)
    all_gather x7, waiting for transfers between devices, gather_rows(): return lax.all_gather(values, 'fsdp', axis=values.ndim - 2, tiled=True)  331 us
    ppermute x11, waiting for transfers between devices, swap_rep(): return lax.ppermute(values, 'rep', [(0, 1), (1, 0)])  237 us
    dot_general x50, matrix products, contract(): lax.dot_general(left_op, right_op, (((left_dim,), (right_dim,)), ((), ())...  236 us
    reduce_scatter x2, waiting for transfers between devices, sum_rows(): return lax.psum_scatter(values, 'fsdp', scatter_dimension=1, tiled=True)  198 us
    unnamed x11, waiting for transfers between devices  65.3 us
  transfers between devices with their start and end apart: 24, of which 15 were waited for; matrix products, arithmetic and copies ran while one was open for 19% of the time, Pallas kernels for 0%

commit v1 on v0

--- a/solution.py
+++ b/solution.py
@@ -8,6 +8,22 @@
 RANK = 256
 CHUNKS = 4
 epsilon = 1e-06
+
+
+def pairwise_exchange(shard, axis, split, join):
+    ways, here = (lax.axis_size(axis), lax.axis_index(axis))
+    width = shard.shape[split] // ways
+    dims = list(shard.shape)
+    dims[split] = width
+    height = dims[join]
+    dims[join] = height * ways
+    full = jnp.zeros(dims, shard.dtype)
+    for mask in range(ways):
+        part = lax.dynamic_slice_in_dim(shard, (here ^ mask) * width, width, axis=split)
+        if mask:
+            part = lax.ppermute(part, axis, [(d, d ^ mask) for d in range(ways)])
+        full = lax.dynamic_update_slice_in_dim(full, part, (here ^ mask) * height, axis=join)
+    return full
 
 
 def rms_scale(values, gain_col):
@@ -115,8 +131,8 @@
     angles = angles_of(query_index[None, :] - before).reshape(count, HD // 2)
     normed, norm_back_one = jax.vjp(rms_scale, hidden_in, gain_two[:, 0])
     normed_low = low(normed)
-    normed_cols = lax.all_to_all(
-        normed_low.reshape(micro, local_len, model_dim), "fsdp", 2, 1, tiled=True
+    normed_cols = pairwise_exchange(
+        normed_low.reshape(micro, local_len, model_dim), "fsdp", 2, 1
     ).reshape(every, attn_rows)
     projected = contract(normed_low, w_proj, 1, 0)
     query_low = low(contract(normed_low, a_q, 1, 0))

time: 1280 us -> 1280 us (level)
  starting transfers between devices: 34.2 us -> 55.9 us
  waiting for transfers between devices: 858 us -> 839 us
    ppermute x0 -> x15, starting transfers between devices: none -> 24.7 us  [pairwise_exchange(): part = lax.ppermute(part, axis, [(d, d ^ mask) for d in range(ways)])]
    all_to_all x1 -> x0, waiting for transfers between devices: 21.9 us -> none  [local(): lax.all_to_all(normed_low.reshape(micro, local_len, model_dim), 'fsdp', 2...]
  transfers between devices with their start and end apart: 24 -> 38, of which waited for: 15 -> 17; matrix products, arithmetic and copies ran while one was open for 19% -> 18% of each run, Pallas kernels for 0% -> 0%
where the time goes in v1:
time: 1280 us; the launch traced here: 1270 us
  waiting for transfers between devices  839 us (66%)
  matrix products  246 us (19%)
  other arithmetic  68.7 us (5%)
  starting transfers between devices  55.9 us (4%)
  local copies, waits for them, and re-layouts  39.6 us (3%)
  between operations  17.1 us (1%)
    all_gather x7, waiting for transfers between devices, gather_rows(): return lax.all_gather(values, 'fsdp', axis=values.ndim - 2, tiled=True)  331 us
    ppermute x11, waiting for transfers between devices, swap_rep(): return lax.ppermute(values, 'rep', [(0, 1), (1, 0)])  236 us
    dot_general x50, matrix products, contract(): lax.dot_general(left_op, right_op, (((left_dim,), (right_dim,)), ((), ())...  236 us
    reduce_scatter x2, waiting for transfers between devices, sum_rows(): return lax.psum_scatter(values, 'fsdp', scatter_dimension=1, tiled=True)  198 us
    unnamed x11, waiting for transfers between devices  64.5 us
  transfers between devices with their start and end apart: 38, of which 17 were waited for; matrix products, arithmetic and copies ran while one was open for 18% of the time, Pallas kernels for 0%

profile of v1, /device:TPU:0, one launch (start us, length us, event | category | flops | bytes accessed | tf_op | source)
XLA Modules:
  0.0 1266.5 jit_solution(8313815986486152845)
XLA Ops:
  13.1 105.5 %all-gather.8.cloned.1.call-done = bf16[2048,3200]{1,0:T(8,128)(2,1)} async-done(((bf16[128,3200]{1,0:T(8,128)(2,1)}), bf16[2048,3200]{1,0:T(8,128)(2,1)}) %all-gather.8.cloned.1.call-update) | async-done | bytes 13107216 | tf_op jit(solution)/shard_map/all_gather | solution.py:82
  136.6 34.2 %all-gather.10.cloned.1.call-done = bf16[2,1024,512]{2,1,0:T(8,128)(2,1)} async-done(((bf16[2,64,512]{2,1,0:T(8,128)(2,1)}), bf16[2,1024,512]{2,1,0:T(8,128)(2,1)}) %all-gather.10.cloned.1.call-update) | async-done | bytes 2097168 | tf_op jit(solution)/shard_map/all_gather | solution.py:82
  178.1 75.3 %all-gather.12.cloned.1.call-done = bf16[2048,2304]{1,0:T(8,128)(2,1)} async-done(((bf16[128,2304]{1,0:T(8,128)(2,1)}), bf16[2048,2304]{1,0:T(8,128)(2,1)}) %all-gather.12.cloned.1.call-update) | async-done | bytes 9437200 | tf_op jit(solution)/shard_map/all_gather | solution.py:82
  253.4 6.4 multiply_reduce_fusion.1
  261.5 66.7 %all-gather.16.cloned.1.call-done = bf16[2,1024,2048]{2,1,0:T(8,128)(2,1)} async-done(((bf16[2,64,2048]{2,1,0:T(8,128)(2,1)}), bf16[2,1024,2048]{2,1,0:T(8,128)(2,1)}) %all-gather.16.cloned.1.call-update) | async-done | bytes 8388624 | tf_op jit(solution)/shard_map/all_gather | solution.py:82
  328.2 7.5 fusion.100
  354.1 49.6 %all-gather.14.cloned.1.call-done = bf16[2,1024,2048]{2,1,0:T(8,128)(2,1)} async-done(((bf16[2,64,2048]{2,1,0:T(8,128)(2,1)}), bf16[2,1024,2048]{2,1,0:T(8,128)(2,1)}) %all-gather.14.cloned.1.call-update) | async-done | bytes 8388624 | tf_op jit(solution)/shard_map/all_gather | solution.py:82
  403.7 7.6 fusion.110
  411.4 7.4 fusion.108
  450.8 14.4 %fusion.13 = f32[2048,2048]{1,0:T(8,128)} fusion(bf16[2048,256]{0,1:T(8,128)(2,1)} %get-tuple-element.27, bf16[2048,256]{0,1:T(8,128)(2,1)} %get-tuple-element.24, bf16[2048,256]{0,1:T(8,128)(2,1)} %get-tuple-element.21, bf16[2048,256]{0,1:T(8,128)(2,1)} %get-tuple-element.18, bf16[1024,3,2048]{2,0,1:T(8,128)(2,1)S(1)} %bitcast.264), kind=kOutput, calls=%fused_computation.22 | convolution fusion | flops 8606711808 | bytes 25165824 | tf_op jit(solution)/shard_map/dot_general | solution.py:60
  465.1 16.3 %add_convert_fusion = bf16[2048,2048]{1,0:T(8,128)(2,1)} fusion(f32[2048,2048]{1,0:T(8,128)} %fusion.13, bf16[2048,256]{0,1:T(8,128)(2,1)} %get-tuple-element.26, bf16[2048,256]{0,1:T(8,128)(2,1)} %get-tuple-element.23, bf16[2048,256]{0,1:T(8,128)(2,1)} %get-tuple-element.20, bf16[2048,256]{0,1:T(8,128)(2,1)S(1)} %copy-done.66, bf16[1024,3,2048]{2,0,1:T(8,128)(2,1)} %param.13), kind=kOutput, calls=%fused_computation.2 | convolution fusion | flops 8615100416 | bytes 33554432 | tf_op jit(solution)/shard_map/dot_general | solution.py:60
  481.5 14.0 %convolution_convert_fusion = bf16[2048,2048]{0,1:T(8,128)(2,1)} fusion(bf16[1024,3,2048]{2,0,1:T(8,128)(2,1)} %param.13, bf16[2048,256]{0,1:T(8,128)(2,1)S(1)} %get-tuple-element.28, bf16[2048,256]{0,1:T(8,128)(2,1)} %get-tuple-element.25, bf16[2048,256]{0,1:T(8,128)(2,1)} %get-tuple-element.22, bf16[2048,256]{0,1:T(8,128)(2,1)} %get-tuple-element.19), kind=kOutput, calls=%fused_computation.12 | convolution fusion | flops 8610906112 | bytes 16777216 | tf_op jit(solution)/shard_map/dot_general | solution.py:60
  495.5 88.1 %reduce-scatter.5.cloned.1.call-done = bf16[2,64,2048]{2,1,0:T(8,128)(2,1)} async-done(((bf16[2,1024,2048]{2,1,0:T(8,128)(2,1)}), bf16[2,64,2048]{2,1,0:T(8,128)(2,1)}) %reduce-scatter.5.cloned.1.call-update) | async-done | bytes 524304 | tf_op jit(solution)/shard_map/reduce_scatter | solution.py:86
  607.8 10.8 pad_maximum_fusion
  618.5 12.8 %copy.50 = bf16[2048,2304]{1,0:T(8,128)(2,1)} copy(bf16[2048,2304]{0,1:T(8,128)(2,1)} %pad_maximum_fusion) | data formatting | bytes 18874368 | tf_op jit(solution)/shard_map/reshape | solution.py:217
  638.3 63.9 %all-reduce.3.cloned.1.call-done = bf16[2,1024,512]{2,0,1:T(2,128)(2,1)} async-done(((bf16[2,1024,512]{2,0,1:T(2,128)(2,1)}), bf16[2,1024,512]{2,0,1:T(2,128)(2,1)}) %all-reduce.3.cloned.1.call-update) | async-done | bytes 2097168
  706.7 110.2 %reduce-scatter.3.cloned.1.call-done = bf16[2,64,2304]{2,1,0:T(8,128)(2,1)} async-done(((bf16[2,1024,2304]{2,1,0:T(8,128)(2,1)}), bf16[2,64,2304]{2,1,0:T(8,128)(2,1)}) %reduce-scatter.3.cloned.1.call-update) | async-done | bytes 589840 | tf_op jit(solution)/shard_map/reduce_scatter | solution.py:86
  836.7 6.0 collective-permute-start.14
  849.6 5.9 fusion.49
  855.6 5.9 fusion.48
  868.5 6.0 fusion.45
  887.3 5.9 fusion.42
  893.2 6.1 fusion.41
  906.9 6.3 fusion.39
  924.9 148.0 %collective-permute-done.25 = bf16[256,256]{1,0:T(8,128)(2,1)S(1)} collective-permute-done((bf16[256,256]{1,0:T(8,128)(2,1)S(1)}, bf16[256,256]{1,0:T(8,128)(2,1)S(1)}, u32[]{:S(2)}, u32[]{:S(2)}) %collective-permute-start.25) | collective-permute-done | bytes 131104 | tf_op jit(solution)/shard_map/ppermute | solution.py:90
  1074.7 67.5 %collective-permute-done.24 = bf16[256,256]{1,0:T(8,128)(2,1)S(1)} collective-permute-done((bf16[256,256]{1,0:T(8,128)(2,1)S(1)}, bf16[256,256]{1,0:T(8,128)(2,1)S(1)}, u32[]{:S(2)}, u32[]{:S(2)}) %collective-permute-start.24) | collective-permute-done | bytes 131104 | tf_op jit(solution)/shard_map/ppermute | solution.py:90
  1168.5 8.8 all-to-all-start.1
  1177.3 17.8 %maximum_bitcast_fusion = f32[1024,3,2048]{2,0,1:T(8,128)} fusion(f32[3,256,2048]{2,1,0:T(8,128)} %convert_add_fusion, f32[3,256,2048]{2,1,0:T(8,128)} %convert_add_fusion.1, f32[3,256,2048]{2,1,0:T(8,128)} %convert_add_fusion.2, f32[3,256,2048]{2,1,0:T(8,128)} %convert_add_fusion.3), kind=kLoop, calls=%fused_computation.1 | loop fusion | flops 18874368 | bytes 50331648 | tf_op jit(solution)/shard_map/transpose | solution.py:284
  1203.6 6.2 fusion.3
  1213.3 6.1 all-to-all-start
  1230.1 6.0 fusion.34
  1242.3 14.3 %collective-permute-done.16 = bf16[128,3328]{1,0:T(8,128)(2,1)S(1)} collective-permute-done((bf16[128,3328]{1,0:T(8,128)(2,1)S(1)}, bf16[128,3328]{1,0:T(8,128)(2,1)S(1)}, u32[]{:S(2)}, u32[]{:S(2)}) %collective-permute-start.16) | collective-permute-done | bytes 852000 | tf_op jit(solution)/shard_map/ppermute | solution.py:90
  (392 shorter events, 242.0 us)
Async XLA Ops:
  7.2 111.4 %all-gather.8.cloned.1.call-start = ((), (), s32[]{:S(2)}) async-start(), calls=%async_computation.4 | async-start | bytes 13926400 | tf_op jit(solution)/shard_map/all_gather | solution.py:82
  12.1 158.8 %all-gather.10.cloned.1.call-start = ((), (), s32[]{:S(2)}) async-start(), calls=%async_computation.5 | async-start | bytes 2228224 | tf_op jit(solution)/shard_map/all_gather | solution.py:82
  131.0 122.4 %all-gather.12.cloned.1.call-start = ((), (), s32[]{:S(2)}) async-start(), calls=%async_computation.6 | async-start | bytes 10027008 | tf_op jit(solution)/shard_map/all_gather | solution.py:82
  131.9 196.3 %all-gather.16.cloned.1.call-start = ((), (), s32[]{:S(2)}) async-start(), calls=%async_computation.9 | async-start | bytes 8912896 | tf_op jit(solution)/shard_map/all_gather | solution.py:82
  132.5 271.2 %all-gather.14.cloned.1.call-start = ((), (), s32[]{:S(2)}) async-start(), calls=%async_computation.7 | async-start | bytes 8912896 | tf_op jit(solution)/shard_map/all_gather | solution.py:82
  261.0 322.6 %reduce-scatter.5.cloned.1.call-start = ((), (), s32[]{:S(2)}) async-start(), calls=%async_computation.10 | async-start | bytes 8912896 | tf_op jit(solution)/shard_map/reduce_scatter | solution.py:86
  481.4 220.7 %all-reduce.3.cloned.1.call-start = ((), (), s32[]{:S(2)}) async-start(), calls=%async_computation.13 | async-start | bytes 4194304
  604.3 212.7 %reduce-scatter.3.cloned.1.call-start = ((), (), s32[]{:S(2)}) async-start(), calls=%async_computation.8 | async-start | bytes 10027008 | tf_op jit(solution)/shard_map/reduce_scatter | solution.py:86
  631.4 565.1 %all-gather.20.cloned.1.call-start = ((), (), s32[]{:S(2)}) async-start(), calls=%async_computation.12 | async-start | bytes 10027008 | tf_op jit(solution)/shard_map/all_gather | solution.py:82
  633.6 593.0 %all-gather.18.cloned.1.call-start = ((), (), s32[]{:S(2)}) async-start(), calls=%async_computation.11 | async-start | bytes 13369344 | tf_op jit(solution)/shard_map/all_gather | solution.py:82
  821.8 6.6 collective-permute-start.4
  823.6 8.6 collective-permute-start.6
  826.2 6.7 collective-permute-start.7
  826.3 8.6 collective-permute-start.8
  828.5 8.2 collective-permute-start.9
  829.3 13.9 %collective-permute-start.10 = (bf16[2,64,128]{2,1,0:T(8,128)(2,1)}, bf16[2,64,128]{2,1,0:T(8,128)(2,1)S(1)}, u32[]{:S(2)}, u32[]{:S(2)}) collective-permute-start(bf16[2,64,128]{2,1,0:T(8,128)(2,1)} %get-tuple-element.40), channel_id=1, source_target_pairs={{0,10},{1,11},{2,8},{3,9},{4,14},{5,15},{6,12},{7,13},{8,2},{9,3},... | collective-permute-start | bytes 98312 | tf_op jit(solution)/shard_map/ppermute | solution.py:24
  832.2 14.2 %collective-permute-start.11 = (bf16[2,64,128]{2,1,0:T(8,128)(2,1)}, bf16[2,64,128]{2,1,0:T(8,128)(2,1)S(1)}, u32[]{:S(2)}, u32[]{:S(2)}) collective-permute-start(bf16[2,64,128]{2,1,0:T(8,128)(2,1)} %get-tuple-element.39), channel_id=1, source_target_pairs={{0,11},{1,10},{2,9},{3,8},{4,15},{5,14},{6,13},{7,12},{8,3},{9,2},... | collective-permute-start | bytes 98312 | tf_op jit(solution)/shard_map/ppermute | solution.py:24
  832.8 13.6 %collective-permute-start.12 = (bf16[2,64,128]{2,1,0:T(8,128)(2,1)}, bf16[2,64,128]{2,1,0:T(8,128)(2,1)S(1)}, u32[]{:S(2)}, u32[]{:S(2)}) collective-permute-start(bf16[2,64,128]{2,1,0:T(8,128)(2,1)} %get-tuple-element.38), channel_id=1, source_target_pairs={{0,12},{1,13},{2,14},{3,15},{4,8},{5,9},{6,10},{7,11},{8,4},{9,5},... | collective-permute-start | bytes 98312 | tf_op jit(solution)/shard_map/ppermute | solution.py:24
  835.0 11.5 collective-permute-start.13
  836.7 9.8 collective-permute-start.14
  843.2 6.4 collective-permute-start.15
  864.2 289.1 %collective-permute-start.21 = (bf16[3,256,2048]{2,1,0:T(8,128)(2,1)S(1)}, bf16[3,256,2048]{2,1,0:T(8,128)(2,1)S(1)}, u32[]{:S(2)}, u32[]{:S(2)}) collective-permute-start(bf16[3,256,2048]{2,1,0:T(8,128)(2,1)S(1)} %pad_maximum_fusion.5), channel_id=1, source_target_pairs={{0,16},{16,0},{1,17},{17,1},{2,18},{18,2},{3,19},{19,3},{4,20},{20... | collective-permute-start | bytes 9437192 | tf_op jit(solution)/shard_map/ppermute | solution.py:90
  880.7 275.9 %collective-permute-start.20 = (bf16[3,256,2048]{2,1,0:T(8,128)(2,1)S(1)}, bf16[3,256,2048]{2,1,0:T(8,128)(2,1)S(1)}, u32[]{:S(2)}, u32[]{:S(2)}) collective-permute-start(bf16[3,256,2048]{2,1,0:T(8,128)(2,1)S(1)} %pad_maximum_fusion.4), channel_id=1, source_target_pairs={{0,16},{16,0},{1,17},{17,1},{2,18},{18,2},{3,19},{19,3},{4,20},{20... | collective-permute-start | bytes 9437192 | tf_op jit(solution)/shard_map/ppermute | solution.py:90
  899.7 260.1 %collective-permute-start.19 = (bf16[3,256,2048]{2,1,0:T(8,128)(2,1)S(1)}, bf16[3,256,2048]{2,1,0:T(8,128)(2,1)S(1)}, u32[]{:S(2)}, u32[]{:S(2)}) collective-permute-start(bf16[3,256,2048]{2,1,0:T(8,128)(2,1)S(1)} %pad_maximum_fusion.3), channel_id=1, source_target_pairs={{0,16},{16,0},{1,17},{17,1},{2,18},{18,2},{3,19},{19,3},{4,20},{20... | collective-permute-start | bytes 9437192 | tf_op jit(solution)/shard_map/ppermute | solution.py:90
  920.7 152.2 %collective-permute-start.25 = (bf16[256,256]{1,0:T(8,128)(2,1)S(1)}, bf16[256,256]{1,0:T(8,128)(2,1)S(1)}, u32[]{:S(2)}, u32[]{:S(2)}) collective-permute-start(bf16[256,256]{1,0:T(8,128)(2,1)S(1)} %convolution_convert_fusion.17), channel_id=1, source_target_pairs={{0,16},{16,0},{1,17},{17,1},{2,18},{18,2},{3,19},{19,3},{4,20},{20... | collective-permute-start | bytes 393224 | tf_op jit(solution)/shard_map/ppermute | solution.py:90
  923.4 239.6 %collective-permute-start.18 = (bf16[3,256,2048]{2,1,0:T(8,128)(2,1)S(1)}, bf16[3,256,2048]{2,1,0:T(8,128)(2,1)S(1)}, u32[]{:S(2)}, u32[]{:S(2)}) collective-permute-start(bf16[3,256,2048]{2,1,0:T(8,128)(2,1)S(1)} %pad_maximum_fusion.2), channel_id=1, source_target_pairs={{0,16},{16,0},{1,17},{17,1},{2,18},{18,2},{3,19},{19,3},{4,20},{20... | collective-permute-start | bytes 9437192 | tf_op jit(solution)/shard_map/ppermute | solution.py:90
  1072.9 69.4 %collective-permute-start.24 = (bf16[256,256]{1,0:T(8,128)(2,1)S(1)}, bf16[256,256]{1,0:T(8,128)(2,1)S(1)}, u32[]{:S(2)}, u32[]{:S(2)}) collective-permute-start(bf16[256,256]{1,0:T(8,128)(2,1)S(1)} %convolution_convert_fusion.18), channel_id=1, source_target_pairs={{0,16},{16,0},{1,17},{17,1},{2,18},{18,2},{3,19},{19,3},{4,20},{20... | collective-permute-start | bytes 393224 | tf_op jit(solution)/shard_map/ppermute | solution.py:90
  1168.5 26.6 %all-to-all-start.1 = ((bf16[16,2,8192]{2,1,0:T(2,128)(2,1)}), bf16[16,2,8192]{2,1,0:T(2,128)(2,1)S(1)}, u32[]{:S(2)}, u32[]{:S(2)}) async-start(bf16[16,2,8192]{2,1,0:T(2,128)(2,1)} %reshape.414), calls=%async_computation.3 | async-start | bytes 1048576 | tf_op jit(solution)/shard_map/all_to_all | solution.py:227
  1202.1 36.2 %collective-permute-start.17 = (bf16[128,2048]{1,0:T(8,128)(2,1)}, bf16[128,2048]{1,0:T(8,128)(2,1)}, u32[]{:S(2)}, u32[]{:S(2)}) collective-permute-start(bf16[128,2048]{1,0:T(8,128)(2,1)} %fusion.56), channel_id=1, source_target_pairs={{0,16},{16,0},{1,17},{17,1},{2,18},{18,2},{3,19},{19,3},{4,20},{20... | collective-permute-start | bytes 1572872 | tf_op jit(solution)/shard_map/ppermute | solution.py:90
  1213.3 12.6 all-to-all-start
  1226.0 11.8 collective-permute-start
  1236.2 20.4 %collective-permute-start.16 = (bf16[128,3328]{1,0:T(8,128)(2,1)S(1)}, bf16[128,3328]{1,0:T(8,128)(2,1)S(1)}, u32[]{:S(2)}, u32[]{:S(2)}) collective-permute-start(bf16[128,3328]{1,0:T(8,128)(2,1)S(1)} %pad_maximum_fusion.9), channel_id=1, source_target_pairs={{0,16},{16,0},{1,17},{17,1},{2,18},{18,2},{3,19},{19,3},{4,20},{20... | collective-permute-start | bytes 2555912 | tf_op jit(solution)/shard_map/ppermute | solution.py:90
  (91 other events, 3374.6 us)
Sparse Core Ops, SparseCore 0:
  12.2 106.3 all-gather.7
  131.1 39.7 all-gather.9
  173.7 79.6 all-gather.11
  255.4 72.7 all-gather.15
  330.8 72.8 all-gather.13
  481.6 101.9 reduce-scatter.4
  604.4 97.7 all-reduce.2
  706.3 110.6 reduce-scatter.2
  819.2 91.7 all-gather.19
  913.2 98.6 all-gather.17
